TPU v7x, 32 devices: a whole 2x2x4 slice. The times are simulated.
32 devices in a mesh: tile: 8 (over z, y), clip: 4 (over x, core).
Axes of the slice: x: 2, y: 2, z: 4, core: 2. Of those that a mesh axis runs over, the one named last changes fastest.
Arguments:
- seq_rows: bfloat16 [32768, 512], P(('tile', 'clip'))
- plan_owner: int32 [32768], P(('tile', 'clip')), may hold values from 0 to 31, as said below
- plan_slot: int32 [32768], P(('tile', 'clip')), may hold values from 0 to 1023, as said below
- live_frames: int32 [4], replicated, may hold values from 1 to 4, as said below
- norm_gain: float32 [512], replicated, may hold values from 0.1 to 1.9
- norm_bias: float32 [512], replicated, may hold values from -3 to 3
- conv_weight: bfloat16 [3, 3, 512, 3, 256], replicated, may hold values from -0.0546875 to 0.0546875
- conv_bias: float32 [256], replicated, may hold values from -3 to 3
Outputs:
- decoded: bfloat16 [4, 8, 4, 8, 32, 256], P('clip', 'tile')
Inputs may be any that keep to these rules, and one draw needn't show every extreme that they name: `plan_owner`: owner o is tile o % 8 of clip o // 8. The 1024 rows of each device send 32 // 2 or 48 rows to each owner, so at most 48, which is reached. The pairs of plan_owner and plan_slot are all distinct: every slot of every owner receives exactly one row. `live_frames`: some clip has all 4 frames live.
All inputs are finite; a program needn't handle non-finite values.
Results may differ from a plain program's by a relative error of at most 0.004.
Values may be sent and summed in bfloat16 or wider, within the bound.
A program may use at most 128 MiB of HBM per device.

v0:
```python
import jax
import jax.numpy as jnp
from jax import lax
from jax.sharding import PartitionSpec as P

GROUPS = 32
LT = 4
TH = 8
TW = 32
GW = 4
EPSILON = 1e-06
HIGHEST = lax.Precision.HIGHEST


def shifted(block, axis, distance):
    devices = range(lax.axis_size(axis))
    route = [(i - distance, i) for i in devices if i - distance in devices]
    return lax.ppermute(block, axis, route)


def neighbour(values, offset):
    return shifted(values, "tile", offset)


def extend(tile_grid, column_tile, grid_cols):
    left_face = neighbour(tile_grid[:, :, -1:], 1)
    right_face = neighbour(tile_grid[:, :, :1], -1)
    left_face = jnp.where(column_tile > 0, left_face, jnp.zeros_like(left_face))
    right_face = jnp.where(column_tile < grid_cols - 1, right_face, jnp.zeros_like(right_face))
    widened = jnp.concatenate([left_face, tile_grid, right_face], axis=2)
    upper_face = neighbour(widened[:, -1:], grid_cols)
    lower_face = neighbour(widened[:, :1], -grid_cols)
    return jnp.concatenate([upper_face, widened, lower_face], axis=1)


def normalize(values, mean_channel, scale_channel, norm_gain, norm_bias):
    normed = (values.astype(jnp.float32) - mean_channel) * scale_channel * norm_gain + norm_bias
    return jax.nn.silu(normed)


def on_device(
    seq_rows, plan_owner, plan_slot, live_frames, norm_gain, norm_bias, conv_weight, conv_bias
):
    row_count, channels = seq_rows.shape
    out_width = conv_bias.shape[0]
    tile_count = lax.axis_size("tile")
    clip_count = lax.axis_size("clip")
    owner_count = tile_count * clip_count
    capacity = 3 * (row_count // owner_count) // 2
    per_group = channels // GROUPS
    plane_size = TH * TW
    voxel_total = float(plane_size * tile_count)
    row_index = jnp.arange(row_count, dtype=jnp.int32)
    owner_table = (plan_owner[:, None] == jnp.arange(owner_count, dtype=jnp.int32)[None, :]).astype(
        jnp.int32
    )
    ranking = jnp.sum((jnp.cumsum(owner_table, axis=0) - 1) * owner_table, axis=1)
    position = plan_owner * capacity + ranking
    my_clip = lax.axis_index("clip")
    my_tile = lax.axis_index("tile")
    frames_live = live_frames[my_clip]
    outgoing = (
        jnp.zeros((owner_count * capacity, channels), jnp.bfloat16).at[position].set(seq_rows)
    )
    slot_list = (
        jnp.full((owner_count * capacity,), row_count, jnp.int32).at[position].set(plan_slot)
    )
    outgoing = outgoing.reshape(clip_count, tile_count, capacity, channels)
    slot_list = slot_list.reshape(clip_count, tile_count, capacity)
    arrived, arrived_slots = (
        lax.all_to_all(
            lax.all_to_all(outgoing, "tile", split_axis=1, concat_axis=1, tiled=True),
            "clip",
            split_axis=0,
            concat_axis=0,
            tiled=True,
        ),
        lax.all_to_all(
            lax.all_to_all(slot_list, "tile", split_axis=1, concat_axis=1, tiled=True),
            "clip",
            split_axis=0,
            concat_axis=0,
            tiled=True,
        ),
    )
    tile_rows = (
        jnp.zeros((row_count, channels), jnp.bfloat16)
        .at[arrived_slots.reshape(-1)]
        .set(arrived.reshape(-1, channels), mode="drop")
    )
    grid_cols = GW
    grid_rows = tile_count // grid_cols
    column_tile = my_tile % grid_cols
    row_tile = my_tile // grid_cols
    live_frame = jnp.arange(LT) < frames_live
    values = tile_rows.astype(jnp.float32)
    live_row = (row_index // plane_size < frames_live).astype(jnp.float32)
    first_sum = jnp.dot(live_row, values, precision=HIGHEST).reshape(GROUPS, per_group).sum(axis=1)
    second_sum = (
        jnp.dot(live_row, values * values, precision=HIGHEST).reshape(GROUPS, per_group).sum(axis=1)
    )
    raw_padded = extend(tile_rows.reshape(LT, TH, TW, channels), column_tile, grid_cols)
    first_sum, second_sum = lax.psum((first_sum, second_sum), "tile")
    count_clip = per_group * frames_live.astype(jnp.float32) * voxel_total
    mean_group = first_sum / count_clip
    scale_group = lax.rsqrt(second_sum / count_clip - mean_group * mean_group + EPSILON)
    mean_channel = jnp.repeat(mean_group, per_group)
    scale_channel = jnp.repeat(scale_group, per_group)
    inside_rows = jnp.arange(TH + 2)
    inside_cols = jnp.arange(TW + 2)
    rows_inside = ((inside_rows > 0) | (row_tile > 0)) & (
        (inside_rows < TH + 1) | (row_tile < grid_rows - 1)
    )
    cols_inside = ((inside_cols > 0) | (column_tile > 0)) & (
        (inside_cols < TW + 1) | (column_tile < grid_cols - 1)
    )
    valid_mask = rows_inside[:, None] & cols_inside[None, :]
    activated = normalize(raw_padded, mean_channel, scale_channel, norm_gain, norm_bias)
    padded = jnp.where(valid_mask[None, :, :, None], activated, 0.0).astype(jnp.bfloat16)
    padded = jnp.concatenate(
        [jnp.zeros((2, TH + 2, TW + 2, channels), jnp.bfloat16), padded], axis=0
    )
    accumulated = jnp.zeros((LT, TH, TW, out_width), jnp.float32)
    for tap_t in range(3):
        for tap_h in range(3):
            slab_rows = padded[tap_t : tap_t + LT, tap_h : tap_h + TH].reshape(-1, channels)
            kernel = conv_weight[tap_t, tap_h].reshape(channels, 3 * out_width)
            product = jnp.dot(slab_rows, kernel, preferred_element_type=jnp.float32)
            product = product.reshape(LT, TH, TW + 2, 3, out_width)
            for tap_w in range(3):
                accumulated = accumulated + product[:, :, tap_w : tap_w + TW, tap_w]
    decoded = jnp.where(live_frame[:, None, None, None], accumulated + conv_bias, 0.0)
    return decoded.astype(jnp.bfloat16)[None, None]


def solution(mesh):
    return jax.shard_map(
        on_device,
        mesh=mesh,
        in_specs=(
            P(("tile", "clip"), None),
            P(("tile", "clip")),
            P(("tile", "clip")),
            P(),
            P(),
            P(),
            P(),
            P(),
        ),
        out_specs=P("clip", "tile", None, None, None, None),
        check_vma=False,
    )
```

profile of v0, /device:TPU:0, one launch (start us, length us, event | category | flops | bytes accessed | tf_op | source)
XLA Modules:
  0.0 185.9 jit_solution(9642833911319196824)
XLA Ops:
  0.7 9.0 %reduce-window.6 = s32[32,8,128]{2,1,0:T(8,128)S(1)} reduce-window(s32[32,8,128]{2,1,0:T(8,128)S(1)} %fusion.53, s32[]{:T(128)} %constant.69.clone.1), window={size=1x1x128 pad=0_0x0_0x127_0}, to_apply=%region_0.0 | reduce-window | flops 4161536 | bytes 262148 | tf_op jit(solution)/shard_map/reduce-window
  11.6 4.5 %scatter_custom_fusion = s32[1536]{0:T(1024)S(1)} fusion(s32[1024]{0:T(1024)S(1)} %compare_select_fusion.1, s32[1024]{0:T(1024)} %param.10, s32[]{:T(128)} %constant.80.clone.1), kind=kCustom, calls=%fused_computation.106 | custom fusion | bytes 6656 | tf_op jit(solution)/shard_map/scatter | solution.py:66
  16.9 7.3 %all-to-all-start = ((s32[8,1,192]{2,1,0:T(1,128)}), s32[8,1,192]{2,1,0:T(1,128)S(1)}, u32[]{:S(2)}, u32[]{:S(2)}) async-start(s32[8,1,192]{2,1,0:T(1,128)} %reshape.525), calls=%async_computation | async-start | bytes 16384 | tf_op jit(solution)/shard_map/all_to_all | solution.py:79
  24.1 6.0 %scatter_custom_fusion.1 = bf16[1536,512]{1,0:T(8,128)(2,1)S(1)} fusion(s32[1024]{0:T(1024)S(1)} %compare_select_fusion.1, bf16[1024,512]{1,0:T(8,128)(2,1)} %param.8, bf16[]{:T(256)} %constant.79.clone.1), kind=kCustom, calls=%fused_computation.80 | custom fusion | bytes 1573376 | tf_op jit(solution)/shard_map/scatter | solution.py:63
  30.2 1.3 copy.91
  31.5 6.0 %all-to-all-start.2 = ((bf16[4,8,48,512]{3,2,0,1:T(8,128)(2,1)}), bf16[4,8,48,512]{3,2,0,1:T(8,128)(2,1)S(1)}, u32[]{:S(2)}, u32[]{:S(2)}) async-start(bf16[4,8,48,512]{3,2,0,1:T(8,128)(2,1)} %copy.91), calls=%async_computation.2 | async-start | bytes 3145728 | tf_op jit(solution)/shard_map/all_to_all | solution.py:72
  39.4 34.5 %all-to-all-done.2 = bf16[4,8,48,512]{3,2,0,1:T(8,128)(2,1)S(1)} async-done(((bf16[4,8,48,512]{3,2,0,1:T(8,128)(2,1)}), bf16[4,8,48,512]{3,2,0,1:T(8,128)(2,1)S(1)}, u32[]{:S(2)}, u32[]{:S(2)}) %all-to-all-start.2) | async-done | bytes 1572896 | tf_op jit(solution)/shard_map/all_to_all | solution.py:72
  73.9 3.2 %all-to-all-start.1 = ((s32[4,1,384]{2,1,0:T(1,128)}), s32[4,1,384]{2,1,0:T(1,128)S(1)}, u32[]{:S(2)}, u32[]{:S(2)}) async-start(s32[4,1,384]{2,1,0:T(1,128)} %reshape.527), calls=%async_computation.1 | async-start | bytes 12288 | tf_op jit(solution)/shard_map/all_to_all | solution.py:78
  79.7 1.3 all-to-all-done.1
  81.0 4.3 %all-to-all-start.3 = ((bf16[4,8,48,512]{3,2,1,0:T(8,128)(2,1)}), bf16[4,8,48,512]{3,2,1,0:T(8,128)(2,1)}, u32[]{:S(2)}, u32[]{:S(2)}) async-start(bf16[4,8,48,512]{3,2,1,0:T(8,128)(2,1)} %copy.92), calls=%async_computation.3 | async-start | bytes 3145728 | tf_op jit(solution)/shard_map/all_to_all | solution.py:71
  85.9 5.5 %fusion.67 = (bf16[1,1,512,3,256]{4,2,3,1,0:T(8,128)(2,1)}, bf16[1,1,512,3,256]{4,2,3,1,0:T(8,128)(2,1)}, bf16[1,1,512,3,256]{4,2,3,1,0:T(8,128)(2,1)}, bf16[1,1...) fusion(bf16[3,3,512,3,256]{4,2,3,1,0:T(8,128)(2,1)} %param.14), kind=kLoop, calls=%fused_computation.122 | loop fusion | bytes 14155776 | tf_op jit(solution)/shard_map/slice | solution.py:127
  91.4 1.4 copy.130
  92.8 2.4 %copy.138 = bf16[1,1,512,3,256]{2,4,3,1,0:T(8,128)(2,1)} copy(bf16[1,1,512,3,256]{4,2,3,1,0:T(8,128)(2,1)} %get-tuple-element.10) | data formatting | bytes 1572864
  95.1 2.3 %copy.137 = bf16[1,1,512,3,256]{2,4,3,1,0:T(8,128)(2,1)} copy(bf16[1,1,512,3,256]{4,2,3,1,0:T(8,128)(2,1)} %get-tuple-element.11) | data formatting | bytes 1572864
  97.4 2.3 %copy.135 = bf16[1,1,512,3,256]{2,4,3,1,0:T(8,128)(2,1)} copy(bf16[1,1,512,3,256]{4,2,3,1,0:T(8,128)(2,1)} %get-tuple-element.12) | data formatting | bytes 1572864
  100.9 1.4 copy.133
  102.3 2.3 %copy.132 = bf16[1,1,512,3,256]{2,4,3,1,0:T(8,128)(2,1)} copy(bf16[1,1,512,3,256]{4,2,3,1,0:T(8,128)(2,1)} %get-tuple-element.15) | data formatting | bytes 1572864
  104.6 2.3 %copy.131 = bf16[1,1,512,3,256]{2,4,3,1,0:T(8,128)(2,1)} copy(bf16[1,1,512,3,256]{4,2,3,1,0:T(8,128)(2,1)} %get-tuple-element.16) | data formatting | bytes 1572864
  109.7 8.0 %scatter_custom_fusion.2 = bf16[1024,512]{1,0:T(8,128)(2,1)S(1)} fusion(s32[1536]{0:T(1024)S(1)} %fusion.54, bf16[1536,512]{1,0:T(8,128)(2,1)} %bitcast.5, bf16[]{:T(256)} %constant.79.clone.1), kind=kCustom, calls=%fused_computation.82 | custom fusion | bytes 1049088 | tf_op jit(solution)/shard_map/scatter | solution.py:89
  118.7 3.3 %collective-permute-start = (bf16[4,8,1,512]{3,2,1,0:T(2,128)(2,1)S(1)}, bf16[4,8,1,512]{3,2,1,0:T(2,128)(2,1)S(1)}, u32[]{:S(2)}, u32[]{:S(2)}) collective-permute-start(bf16[4,8,1,512]{3,2,1,0:T(2,128)(2,1)S(1)} %get-tuple-element.20), channel_id=1, source_target_pairs={{0,4},{4,8},{8,12},{12,16},{16,20},{20,24},{24,28},{1,5},{5,9},{9,... | collective-permute-start | bytes 98312 | tf_op jit(solution)/shard_map/ppermute | solution.py:18
  122.7 1.3 collective-permute-start.1
  124.0 20.7 %all-reduce.1 = (f32[32]{0:T(128)S(1)}, f32[32]{0:T(128)S(1)}) all-reduce(f32[32]{0:T(128)S(1)} %reduce_sum.28, f32[32]{0:T(128)S(1)} %reduce_sum.29), channel_id=1, replica_groups=mesh['tile'=8,'clip'=4] {'tile'}, use_global_device_ids=true, to_apply=%region_7.8 | all-reduce | flops 64 | bytes 512 | tf_op jit(solution)/shard_map/psum | solution.py:103
  145.0 1.3 collective-permute-start.2
  146.3 1.3 collective-permute-start.3
  149.1 6.4 %collective-permute-done.3 = bf16[4,1,34,512]{3,2,1,0:T(8,128)(2,1)S(1)} collective-permute-done((bf16[4,1,34,512]{3,2,1,0:T(8,128)(2,1)S(1)}, bf16[4,1,34,512]{3,2,1,0:T(8,128)(2,1)S(1)}, u32[]{:S(2)}, u32[]{:S(2)}) %collective-permute-start.3) | collective-permute-done | bytes 139296 | tf_op jit(solution)/shard_map/ppermute | solution.py:18
  155.5 2.5 %select_convert_fusion = bf16[4,10,34,512]{3,2,1,0:T(8,128)(2,1)S(1)} fusion(bf16[4,1,34,512]{3,2,1,0:T(8,128)(2,1)S(1)} %collective-permute-done.3, bf16[4,8,1,512]{3,2,1,0:T(2,128)(2,1)S(1)} %broadcast_select_fusion, bf16[4,8,32,512]{3,2,1,0:T(8,128)(2,1)S(1)} %bitcast.241, bf16[4,8,1,512]{3,2,1,0:T(2,128)(2,1)S(1)} %broadcast_select_fusion.1, ...), kind=kLoop, calls=%fused_computation.3 | loop fusion | flops 13926400 | bytes 2793812 | tf_op jit(solution)/shard_map/convert_element_type | solution.py:119
  158.0 2.5 %fusion.21 = f32[4,8,34,3,256]{4,2,1,0,3:T(8,128)S(1)} fusion(bf16[4,10,34,512]{3,2,1,0:T(8,128)(2,1)S(1)} %select_convert_fusion, bf16[1,1,512,3,256]{2,4,3,1,0:T(8,128)(2,1)} %copy.139), kind=kOutput, calls=%fused_computation.26 | convolution fusion | flops 855638016 | bytes 5439488 | tf_op jit(solution)/shard_map/dot_general | solution.py:128
  165.6 3.1 %fusion.19 = f32[4,8,34,3,256]{4,2,3,1,0:T(8,128)} fusion(bf16[4,10,34,512]{3,2,1,0:T(8,128)(2,1)S(1)} %select_convert_fusion, bf16[1,1,512,3,256]{2,4,3,1,0:T(8,128)(2,1)S(1)} %copy-done), kind=kOutput, calls=%fused_computation.24 | convolution fusion | flops 855638016 | bytes 5521408 | tf_op jit(solution)/shard_map/dot_general | solution.py:128
  168.7 3.2 %fusion.23 = f32[4,8,34,3,256]{4,2,1,0,3:T(8,128)} fusion(bf16[4,10,34,512]{3,2,1,0:T(8,128)(2,1)S(1)} %select_convert_fusion, bf16[1,1,512,3,256]{2,4,3,1,0:T(8,128)(2,1)S(1)} %copy-done.5), kind=kOutput, calls=%fused_computation.30 | convolution fusion | flops 855638016 | bytes 5439488 | tf_op jit(solution)/shard_map/dot_general | solution.py:128
  171.9 3.2 %fusion.22 = f32[4,8,34,3,256]{4,2,1,0,3:T(8,128)} fusion(bf16[4,10,34,512]{3,2,1,0:T(8,128)(2,1)S(1)} %select_convert_fusion, bf16[1,1,512,3,256]{2,4,3,1,0:T(8,128)(2,1)S(1)} %copy-done.4), kind=kOutput, calls=%fused_computation.28 | convolution fusion | flops 855638016 | bytes 5439488 | tf_op jit(solution)/shard_map/dot_general | solution.py:128
  175.1 3.2 %fusion.4 = f32[4,8,34,3,256]{4,2,3,1,0:T(8,128)} fusion(bf16[4,10,34,512]{3,2,1,0:T(8,128)(2,1)S(1)} %select_convert_fusion, bf16[1,1,512,3,256]{2,4,3,1,0:T(8,128)(2,1)S(1)} %copy.130), kind=kOutput, calls=%fused_computation.14 | convolution fusion | flops 855638016 | bytes 5521408 | tf_op jit(solution)/shard_map/dot_general | solution.py:128
  178.3 7.6 %fusion.27 = bf16[1,1,4,8,32,256]{5,4,3,2,1,0:T(8,128)(2,1)} fusion(f32[4,8,34,3,256]{4,2,1,0,3:T(8,128)S(1)} %fusion.21, f32[4,8,34,3,256]{4,2,1,0,3:T(8,128)} %fusion.22, f32[4,8,34,3,256]{4,2,1,0,3:T(8,128)} %fusion.23, f32[4,8,34,3,256]{4,2,3,1,0:T(8,128)} %fusion.19, f32[4,8,34,3,256]{4,2,3,1,0:T(8,128)S(1)} %fusion.16, ...), kind=kLoop, calls=%fused_computation.35 | loop fusion | flops 7602176 | bytes 28836868 | tf_op jit(solution)/shard_map/convert_element_type | solution.py:133
  (75 shorter events, 20.1 us)
Async XLA Ops:
  16.9 14.6 %all-to-all-start = ((s32[8,1,192]{2,1,0:T(1,128)}), s32[8,1,192]{2,1,0:T(1,128)S(1)}, u32[]{:S(2)}, u32[]{:S(2)}) async-start(s32[8,1,192]{2,1,0:T(1,128)} %reshape.525), calls=%async_computation | async-start | bytes 16384 | tf_op jit(solution)/shard_map/all_to_all | solution.py:79
  30.2 47.0 %copy-start.9 = (s32[4]{0:T(128)S(1)}, s32[4]{0:T(128)}, u32[]{:S(2)}) copy-start(s32[4]{0:T(128)} %param.11) | copy-start | bytes 52
  31.5 42.4 %all-to-all-start.2 = ((bf16[4,8,48,512]{3,2,0,1:T(8,128)(2,1)}), bf16[4,8,48,512]{3,2,0,1:T(8,128)(2,1)S(1)}, u32[]{:S(2)}, u32[]{:S(2)}) async-start(bf16[4,8,48,512]{3,2,0,1:T(8,128)(2,1)} %copy.91), calls=%async_computation.2 | async-start | bytes 3145728 | tf_op jit(solution)/shard_map/all_to_all | solution.py:72
  73.9 7.0 %all-to-all-start.1 = ((s32[4,1,384]{2,1,0:T(1,128)}), s32[4,1,384]{2,1,0:T(1,128)S(1)}, u32[]{:S(2)}, u32[]{:S(2)}) async-start(s32[4,1,384]{2,1,0:T(1,128)} %reshape.527), calls=%async_computation.1 | async-start | bytes 12288 | tf_op jit(solution)/shard_map/all_to_all | solution.py:78
  81.0 28.7 %all-to-all-start.3 = ((bf16[4,8,48,512]{3,2,1,0:T(8,128)(2,1)}), bf16[4,8,48,512]{3,2,1,0:T(8,128)(2,1)}, u32[]{:S(2)}, u32[]{:S(2)}) async-start(bf16[4,8,48,512]{3,2,1,0:T(8,128)(2,1)} %copy.92), calls=%async_computation.3 | async-start | bytes 3145728 | tf_op jit(solution)/shard_map/all_to_all | solution.py:71
  109.7 45.9 %copy-start.6 = (f32[512]{0:T(512)S(1)}, f32[512]{0:T(512)}, u32[]{:S(2)}) copy-start(f32[512]{0:T(512)} %param.13) | copy-start | bytes 6148
  109.7 45.9 %copy-start.7 = (f32[512]{0:T(512)S(1)}, f32[512]{0:T(512)}, u32[]{:S(2)}) copy-start(f32[512]{0:T(512)} %param.12) | copy-start | bytes 6148
  118.7 26.0 %collective-permute-start = (bf16[4,8,1,512]{3,2,1,0:T(2,128)(2,1)S(1)}, bf16[4,8,1,512]{3,2,1,0:T(2,128)(2,1)S(1)}, u32[]{:S(2)}, u32[]{:S(2)}) collective-permute-start(bf16[4,8,1,512]{3,2,1,0:T(2,128)(2,1)S(1)} %get-tuple-element.20), channel_id=1, source_target_pairs={{0,4},{4,8},{8,12},{12,16},{16,20},{20,24},{24,28},{1,5},{5,9},{9,... | collective-permute-start | bytes 98312 | tf_op jit(solution)/shard_map/ppermute | solution.py:18
  122.7 22.1 %collective-permute-start.1 = (bf16[4,8,1,512]{3,2,1,0:T(2,128)(2,1)S(1)}, bf16[4,8,1,512]{3,2,1,0:T(2,128)(2,1)S(1)}, u32[]{:S(2)}, u32[]{:S(2)}) collective-permute-start(bf16[4,8,1,512]{3,2,1,0:T(2,128)(2,1)S(1)} %get-tuple-element.21), channel_id=1, source_target_pairs={{4,0},{8,4},{12,8},{16,12},{20,16},{24,20},{28,24},{5,1},{9,5},{13... | collective-permute-start | bytes 98312 | tf_op jit(solution)/shard_map/ppermute | solution.py:18
  145.0 4.2 %collective-permute-start.2 = (bf16[4,1,34,512]{3,2,1,0:T(8,128)(2,1)S(1)}, bf16[4,1,34,512]{3,2,1,0:T(8,128)(2,1)S(1)}, u32[]{:S(2)}, u32[]{:S(2)}) collective-permute-start(bf16[4,1,34,512]{3,2,1,0:T(8,128)(2,1)S(1)} %get-tuple-element.18), channel_id=1, source_target_pairs={{0,16},{4,20},{8,24},{12,28},{1,17},{5,21},{9,25},{13,29},{2,18},{... | collective-permute-start | bytes 417800 | tf_op jit(solution)/shard_map/ppermute | solution.py:18
  146.3 9.2 %collective-permute-start.3 = (bf16[4,1,34,512]{3,2,1,0:T(8,128)(2,1)S(1)}, bf16[4,1,34,512]{3,2,1,0:T(8,128)(2,1)S(1)}, u32[]{:S(2)}, u32[]{:S(2)}) collective-permute-start(bf16[4,1,34,512]{3,2,1,0:T(8,128)(2,1)S(1)} %get-tuple-element.19), channel_id=1, source_target_pairs={{16,0},{20,4},{24,8},{28,12},{17,1},{21,5},{25,9},{29,13},{18,2},{... | collective-permute-start | bytes 417800 | tf_op jit(solution)/shard_map/ppermute | solution.py:18
  158.0 2.5 %copy-start.3 = (bf16[1,1,512,3,256]{2,4,3,1,0:T(8,128)(2,1)S(1)}, bf16[1,1,512,3,256]{2,4,3,1,0:T(8,128)(2,1)}, u32[]{:S(2)}) copy-start(bf16[1,1,512,3,256]{2,4,3,1,0:T(8,128)(2,1)} %copy.131) | copy-start | bytes 2359300
  160.5 1.3 copy-start.2
  163.0 1.3 copy-start.1
  164.3 1.3 copy-start
  165.6 3.2 %copy-start.5 = (bf16[1,1,512,3,256]{2,4,3,1,0:T(8,128)(2,1)S(1)}, bf16[1,1,512,3,256]{2,4,3,1,0:T(8,128)(2,1)}, u32[]{:S(2)}) copy-start(bf16[1,1,512,3,256]{2,4,3,1,0:T(8,128)(2,1)} %copy.137) | copy-start | bytes 2359300
  168.7 3.2 %copy-start.4 = (bf16[1,1,512,3,256]{2,4,3,1,0:T(8,128)(2,1)S(1)}, bf16[1,1,512,3,256]{2,4,3,1,0:T(8,128)(2,1)}, u32[]{:S(2)}) copy-start(bf16[1,1,512,3,256]{2,4,3,1,0:T(8,128)(2,1)} %copy.138) | copy-start | bytes 2359300
  175.1 3.2 %copy-start.8 = (f32[256]{0:T(256)S(1)}, f32[256]{0:T(256)}, u32[]{:S(2)}) copy-start(f32[256]{0:T(256)} %param.15) | copy-start | bytes 3076
where the time goes:
time: 187 us; the launch traced here: 186 us
  local copies, waits for them, and re-layouts  47 us (25%)
  waiting for transfers between devices  43.4 us (23%)
  starting transfers between devices  28.1 us (15%)
  other arithmetic  24.4 us (13%)
  matrix products  21.3 us (11%)
  blocking collectives  20.7 us (11%)
    all_to_all x1, waiting for transfers between devices, on_device(): lax.all_to_all(outgoing, 'tile', split_axis=1, concat_axis=1, tiled=True)  34.5 us
    psum x1, blocking collectives, on_device(): first_sum, second_sum = lax.psum((first_sum, second_sum), 'tile')  20.7 us
    dot_general x9, matrix products, on_device(): product = jnp.dot(slab_rows, kernel, preferred_element_type=jnp.float32)  20.2 us
    unnamed x33, local copies, waits for them, and re-layouts  18.3 us
    another operation x2, other arithmetic  9.04 us
    scatter x1, local copies, waits for them, and re-layouts, on_device(): tile_rows = jnp.zeros((row_count, channels), jnp.bfloat16).at[arrived_slo...  8 us
    ppermute x4, waiting for transfers between devices, shifted(): return lax.ppermute(block, axis, route)  7.63 us
    convert_element_type x1, other arithmetic, on_device(): return decoded.astype(jnp.bfloat16)[None, None]  7.58 us
  transfers between devices with their start and end apart: 8, of which 4 were waited for; matrix products, arithmetic and copies ran while one was open for 20% of the time, Pallas kernels for 0%

commit v1 on v0

--- a/solution.py
+++ b/solution.py
@@ -41,6 +41,24 @@
 def on_device(
     seq_rows, plan_owner, plan_slot, live_frames, norm_gain, norm_bias, conv_weight, conv_bias
 ):
+
+    def divide_spots_here(vec, dim_i, k_dim):
+        mid_arr, all_values = (lax.axis_size("tile"), lax.axis_index("tile"))
+        newest = vec.shape[dim_i] // mid_arr
+        small = list(vec.shape)
+        small[dim_i] = newest
+        wide_out = small[k_dim]
+        small[k_dim] = wide_out * mid_arr
+        r2 = jnp.zeros(small, vec.dtype)
+        for u in range(mid_arr):
+            after = lax.dynamic_slice_in_dim(vec, (all_values ^ u) * newest, newest, axis=dim_i)
+            if u:
+                after = lax.ppermute(
+                    after, "tile", list(map(lambda kk: (kk, kk ^ u), range(mid_arr)))
+                )
+            r2 = lax.dynamic_update_slice_in_dim(r2, after, (all_values ^ u) * wide_out, axis=k_dim)
+        return r2
+
     row_count, channels = seq_rows.shape
     out_width = conv_bias.shape[0]
     tile_count = lax.axis_size("tile")
@@ -76,11 +94,7 @@
             tiled=True,
         ),
         lax.all_to_all(
-            lax.all_to_all(slot_list, "tile", split_axis=1, concat_axis=1, tiled=True),
-            "clip",
-            split_axis=0,
-            concat_axis=0,
-            tiled=True,
+            divide_spots_here(slot_list, 1, 1), "clip", split_axis=0, concat_axis=0, tiled=True
         ),
     )
     tile_rows = (

time: 187 us -> 179 us (0.957)
  waiting for transfers between devices: 43.4 us -> 29.9 us
  starting transfers between devices: 28.1 us -> 33.7 us
    all_to_all x1, waiting for transfers between devices: 34.5 us -> 0.01 us  [on_device(): lax.all_to_all(outgoing, 'tile', split_axis=1, concat_axis=1, tiled=True)]
    ppermute x0 -> x7, waiting for transfers between devices: none -> 21.1 us  [divide_spots_here(): lax.ppermute(after, 'tile', list(map(lambda kk: (kk, kk ^ u), range(mid_a...]
    ppermute x0 -> x7, starting transfers between devices: none -> 12.3 us  [divide_spots_here(): lax.ppermute(after, 'tile', list(map(lambda kk: (kk, kk ^ u), range(mid_a...]
    all_to_all x2 -> x1, starting transfers between devices: 10.5 us -> 3.25 us  [on_device(): lax.all_to_all(divide_spots_here(slot_list, 1, 1), 'clip', split_axis=0,...]
    unnamed x33 -> x31, local copies, waits for them, and re-layouts: 18.3 us -> 17.5 us
  transfers between devices with their start and end apart: 8 -> 14, of which waited for: 4 -> 6; matrix products, arithmetic and copies ran while one was open for 20% -> 19% of each run, Pallas kernels for 0% -> 0%
where the time goes in v1:
time: 179 us; the launch traced here: 178 us
  local copies, waits for them, and re-layouts  46.7 us (26%)
  starting transfers between devices  33.7 us (19%)
  waiting for transfers between devices  29.9 us (17%)
  other arithmetic  23.9 us (13%)
  matrix products  21.3 us (12%)
  blocking collectives  21.2 us (12%)
    psum x1, blocking collectives, on_device(): first_sum, second_sum = lax.psum((first_sum, second_sum), 'tile')  21.2 us
    ppermute x7, waiting for transfers between devices, divide_spots_here(): lax.ppermute(after, 'tile', list(map(lambda kk: (kk, kk ^ u), range(mid_a...  21.1 us
    dot_general x9, matrix products, on_device(): product = jnp.dot(slab_rows, kernel, preferred_element_type=jnp.float32)  20.1 us
    unnamed x31, local copies, waits for them, and re-layouts  17.5 us
    ppermute x7, starting transfers between devices, divide_spots_here(): lax.ppermute(after, 'tile', list(map(lambda kk: (kk, kk ^ u), range(mid_a...  12.3 us
    another operation x2, other arithmetic  9.04 us
    scatter x1, local copies, waits for them, and re-layouts, on_device(): tile_rows = jnp.zeros((row_count, channels), jnp.bfloat16).at[arrived_slo...  8.18 us
    ppermute x4, waiting for transfers between devices, shifted(): return lax.ppermute(block, axis, route)  7.63 us
  transfers between devices with their start and end apart: 14, of which 6 were waited for; matrix products, arithmetic and copies ran while one was open for 19% of the time, Pallas kernels for 0%

profile of v1, /device:TPU:0, one launch (start us, length us, event | category | flops | bytes accessed | tf_op | source)
XLA Modules:
  0.0 177.7 jit_solution(5816231173948608768)
XLA Ops:
  0.7 9.0 %reduce-window.6 = s32[32,8,128]{2,1,0:T(8,128)S(1)} reduce-window(s32[32,8,128]{2,1,0:T(8,128)S(1)} %fusion.53, s32[]{:T(128)} %constant.38.clone.1), window={size=1x1x128 pad=0_0x0_0x127_0}, to_apply=%region_0.0 | reduce-window | flops 4161536 | bytes 262148 | tf_op jit(solution)/shard_map/reduce-window
  11.6 6.0 %scatter_custom_fusion.1 = bf16[1536,512]{1,0:T(8,128)(2,1)S(1)} fusion(s32[1024]{0:T(1024)S(1)} %compare_select_fusion.1, bf16[1024,512]{1,0:T(8,128)(2,1)} %param.8, bf16[]{:T(256)} %constant.85.clone.1), kind=kCustom, calls=%fused_computation.80 | custom fusion | bytes 1573376 | tf_op jit(solution)/shard_map/scatter | solution.py:81
  19.0 7.4 %all-to-all-start.1 = ((bf16[4,8,48,512]{3,2,0,1:T(8,128)(2,1)}), bf16[4,8,48,512]{3,2,0,1:T(8,128)(2,1)S(1)}, u32[]{:S(2)}, u32[]{:S(2)}) async-start(bf16[4,8,48,512]{3,2,0,1:T(8,128)(2,1)} %copy.64), calls=%async_computation.1 | async-start | bytes 3145728 | tf_op jit(solution)/shard_map/all_to_all | solution.py:90
  26.4 4.5 %scatter_custom_fusion = s32[1536]{0:T(1024)S(1)} fusion(s32[1024]{0:T(1024)S(1)} %compare_select_fusion.1, s32[1024]{0:T(1024)} %param.10, s32[]{:T(128)} %constant.86.clone.1), kind=kCustom, calls=%fused_computation.106 | custom fusion | bytes 6656 | tf_op jit(solution)/shard_map/scatter | solution.py:84
  31.0 2.1 %collective-permute-start.1 = (s32[4,1,48]{2,1,0:T(1,128)S(1)}, s32[4,1,48]{2,1,0:T(1,128)S(1)}, u32[]{:S(2)}, u32[]{:S(2)}) collective-permute-start(s32[4,1,48]{2,1,0:T(1,128)S(1)} %get-tuple-element.27), channel_id=1, source_target_pairs={{0,8},{4,12},{8,0},{12,4},{16,24},{20,28},{24,16},{28,20},{1,9},{5... | collective-permute-start | bytes 2312 | tf_op jit(solution)/shard_map/ppermute | solution.py:56
  33.0 1.5 collective-permute-start
  34.5 2.4 %collective-permute-start.4 = (s32[4,1,48]{2,1,0:T(1,128)S(1)}, s32[4,1,48]{2,1,0:T(1,128)S(1)}, u32[]{:S(2)}, u32[]{:S(2)}) collective-permute-start(s32[4,1,48]{2,1,0:T(1,128)S(1)} %get-tuple-element.24), channel_id=1, source_target_pairs={{0,20},{4,16},{8,28},{12,24},{16,4},{20,0},{24,12},{28,8},{1,21},{... | collective-permute-start | bytes 2312 | tf_op jit(solution)/shard_map/ppermute | solution.py:56
  36.9 1.5 collective-permute-start.2
  38.9 13.9 %collective-permute-done.1 = s32[4,1,48]{2,1,0:T(1,128)S(1)} collective-permute-done((s32[4,1,48]{2,1,0:T(1,128)S(1)}, s32[4,1,48]{2,1,0:T(1,128)S(1)}, u32[]{:S(2)}, u32[]{:S(2)}) %collective-permute-start.1) | collective-permute-done | bytes 800 | tf_op jit(solution)/shard_map/ppermute | solution.py:56
  52.8 2.9 %collective-permute-start.5 = (s32[4,1,48]{2,1,0:T(1,128)S(1)}, s32[4,1,48]{2,1,0:T(1,128)S(1)}, u32[]{:S(2)}, u32[]{:S(2)}) collective-permute-start(s32[4,1,48]{2,1,0:T(1,128)S(1)} %get-tuple-element.23), channel_id=1, source_target_pairs={{0,24},{4,28},{8,16},{12,20},{16,8},{20,12},{24,0},{28,4},{1,25},{... | collective-permute-start | bytes 2312 | tf_op jit(solution)/shard_map/ppermute | solution.py:56
  55.7 1.5 collective-permute-start.6
  57.3 6.4 %collective-permute-done.3 = s32[4,1,48]{2,1,0:T(1,128)S(1)} collective-permute-done((s32[4,1,48]{2,1,0:T(1,128)S(1)}, s32[4,1,48]{2,1,0:T(1,128)S(1)}, u32[]{:S(2)}, u32[]{:S(2)}) %collective-permute-start.3) | collective-permute-done | bytes 800 | tf_op jit(solution)/shard_map/ppermute | solution.py:56
  65.3 3.2 %all-to-all-start = ((s32[4,1,384]{2,1,0:T(1,128)}), s32[4,1,384]{2,1,0:T(1,128)S(1)}, u32[]{:S(2)}, u32[]{:S(2)}) async-start(s32[4,1,384]{2,1,0:T(1,128)} %reshape.525), calls=%async_computation | async-start | bytes 12288 | tf_op jit(solution)/shard_map/all_to_all | solution.py:96
  72.3 4.3 %all-to-all-start.2 = ((bf16[4,8,48,512]{3,2,1,0:T(8,128)(2,1)}), bf16[4,8,48,512]{3,2,1,0:T(8,128)(2,1)}, u32[]{:S(2)}, u32[]{:S(2)}) async-start(bf16[4,8,48,512]{3,2,1,0:T(8,128)(2,1)} %copy.65), calls=%async_computation.2 | async-start | bytes 3145728 | tf_op jit(solution)/shard_map/all_to_all | solution.py:89
  77.4 5.4 %fusion.67 = (bf16[1,1,512,3,256]{4,2,3,1,0:T(8,128)(2,1)}, bf16[1,1,512,3,256]{4,2,3,1,0:T(8,128)(2,1)}, bf16[1,1,512,3,256]{4,2,3,1,0:T(8,128)(2,1)}, bf16[1,1...) fusion(bf16[3,3,512,3,256]{4,2,3,1,0:T(8,128)(2,1)} %param.14), kind=kLoop, calls=%fused_computation.130 | loop fusion | bytes 14155776 | tf_op jit(solution)/shard_map/slice | solution.py:141
  84.2 2.4 %copy.111 = bf16[1,1,512,3,256]{2,4,3,1,0:T(8,128)(2,1)} copy(bf16[1,1,512,3,256]{4,2,3,1,0:T(8,128)(2,1)} %get-tuple-element.10) | data formatting | bytes 1572864
  86.6 2.3 %copy.110 = bf16[1,1,512,3,256]{2,4,3,1,0:T(8,128)(2,1)} copy(bf16[1,1,512,3,256]{4,2,3,1,0:T(8,128)(2,1)} %get-tuple-element.11) | data formatting | bytes 1572864
  88.9 2.3 %copy.108 = bf16[1,1,512,3,256]{2,4,3,1,0:T(8,128)(2,1)} copy(bf16[1,1,512,3,256]{4,2,3,1,0:T(8,128)(2,1)} %get-tuple-element.12) | data formatting | bytes 1572864
  92.3 1.4 copy.106
  93.7 2.3 %copy.105 = bf16[1,1,512,3,256]{2,4,3,1,0:T(8,128)(2,1)} copy(bf16[1,1,512,3,256]{4,2,3,1,0:T(8,128)(2,1)} %get-tuple-element.15) | data formatting | bytes 1572864
  96.0 2.3 %copy.104 = bf16[1,1,512,3,256]{2,4,3,1,0:T(8,128)(2,1)} copy(bf16[1,1,512,3,256]{4,2,3,1,0:T(8,128)(2,1)} %get-tuple-element.16) | data formatting | bytes 1572864
  101.7 8.2 %scatter_custom_fusion.2 = bf16[1024,512]{1,0:T(8,128)(2,1)S(1)} fusion(s32[1536]{0:T(1024)S(1)} %fusion.54, bf16[1536,512]{1,0:T(8,128)(2,1)} %bitcast.5, bf16[]{:T(256)} %constant.85.clone.1), kind=kCustom, calls=%fused_computation.82 | custom fusion | bytes 1049088 | tf_op jit(solution)/shard_map/scatter | solution.py:103
  110.9 2.5 %collective-permute-start.7 = (bf16[4,8,1,512]{3,2,1,0:T(2,128)(2,1)S(1)}, bf16[4,8,1,512]{3,2,1,0:T(2,128)(2,1)S(1)}, u32[]{:S(2)}, u32[]{:S(2)}) collective-permute-start(bf16[4,8,1,512]{3,2,1,0:T(2,128)(2,1)S(1)} %get-tuple-element.20), channel_id=1, source_target_pairs={{0,4},{4,8},{8,12},{12,16},{16,20},{20,24},{24,28},{1,5},{5,9},{9,... | collective-permute-start | bytes 98312 | tf_op jit(solution)/shard_map/ppermute | solution.py:18
  115.4 21.2 %all-reduce.1 = (f32[32]{0:T(128)S(1)}, f32[32]{0:T(128)S(1)}) all-reduce(f32[32]{0:T(128)S(1)} %reduce_sum.28, f32[32]{0:T(128)S(1)} %reduce_sum.29), channel_id=1, replica_groups=mesh['tile'=8,'clip'=4] {'tile'}, use_global_device_ids=true, to_apply=%region_7.8 | all-reduce | flops 64 | bytes 512 | tf_op jit(solution)/shard_map/psum | solution.py:117
  141.0 6.4 %collective-permute-done.10 = bf16[4,1,34,512]{3,2,1,0:T(8,128)(2,1)S(1)} collective-permute-done((bf16[4,1,34,512]{3,2,1,0:T(8,128)(2,1)S(1)}, bf16[4,1,34,512]{3,2,1,0:T(8,128)(2,1)S(1)}, u32[]{:S(2)}, u32[]{:S(2)}) %collective-permute-start.10) | collective-permute-done | bytes 139296 | tf_op jit(solution)/shard_map/ppermute | solution.py:18
  147.4 2.5 %select_convert_fusion = bf16[4,10,34,512]{3,2,1,0:T(8,128)(2,1)S(1)} fusion(bf16[4,1,34,512]{3,2,1,0:T(8,128)(2,1)S(1)} %collective-permute-done.10, bf16[4,8,1,512]{3,2,1,0:T(2,128)(2,1)S(1)} %broadcast_select_fusion, bf16[4,8,32,512]{3,2,1,0:T(8,128)(2,1)S(1)} %bitcast.237, bf16[4,8,1,512]{3,2,1,0:T(2,128)(2,1)S(1)} %broadcast_select_fusion.1, ...), kind=kLoop, calls=%fused_computation.3 | loop fusion | flops 13926400 | bytes 2793812 | tf_op jit(solution)/shard_map/convert_element_type | solution.py:133
  149.9 2.5 %fusion.21 = f32[4,8,34,3,256]{4,2,1,0,3:T(8,128)S(1)} fusion(bf16[4,10,34,512]{3,2,1,0:T(8,128)(2,1)S(1)} %select_convert_fusion, bf16[1,1,512,3,256]{2,4,3,1,0:T(8,128)(2,1)} %copy.112), kind=kOutput, calls=%fused_computation.26 | convolution fusion | flops 855638016 | bytes 5439488 | tf_op jit(solution)/shard_map/dot_general | solution.py:142
  157.5 3.1 %fusion.19 = f32[4,8,34,3,256]{4,2,3,1,0:T(8,128)} fusion(bf16[4,10,34,512]{3,2,1,0:T(8,128)(2,1)S(1)} %select_convert_fusion, bf16[1,1,512,3,256]{2,4,3,1,0:T(8,128)(2,1)S(1)} %copy-done), kind=kOutput, calls=%fused_computation.24 | convolution fusion | flops 855638016 | bytes 5521408 | tf_op jit(solution)/shard_map/dot_general | solution.py:142
  160.6 3.1 %fusion.23 = f32[4,8,34,3,256]{4,2,1,0,3:T(8,128)} fusion(bf16[4,10,34,512]{3,2,1,0:T(8,128)(2,1)S(1)} %select_convert_fusion, bf16[1,1,512,3,256]{2,4,3,1,0:T(8,128)(2,1)S(1)} %copy-done.5), kind=kOutput, calls=%fused_computation.30 | convolution fusion | flops 855638016 | bytes 5439488 | tf_op jit(solution)/shard_map/dot_general | solution.py:142
  163.7 3.2 %fusion.22 = f32[4,8,34,3,256]{4,2,1,0,3:T(8,128)} fusion(bf16[4,10,34,512]{3,2,1,0:T(8,128)(2,1)S(1)} %select_convert_fusion, bf16[1,1,512,3,256]{2,4,3,1,0:T(8,128)(2,1)S(1)} %copy-done.4), kind=kOutput, calls=%fused_computation.28 | convolution fusion | flops 855638016 | bytes 5439488 | tf_op jit(solution)/shard_map/dot_general | solution.py:142
  167.0 3.2 %fusion.4 = f32[4,8,34,3,256]{4,2,3,1,0:T(8,128)} fusion(bf16[4,10,34,512]{3,2,1,0:T(8,128)(2,1)S(1)} %select_convert_fusion, bf16[1,1,512,3,256]{2,4,3,1,0:T(8,128)(2,1)S(1)} %copy.103), kind=kOutput, calls=%fused_computation.14 | convolution fusion | flops 855638016 | bytes 5521408 | tf_op jit(solution)/shard_map/dot_general | solution.py:142
  170.2 7.6 %fusion.27 = bf16[1,1,4,8,32,256]{5,4,3,2,1,0:T(8,128)(2,1)} fusion(f32[4,8,34,3,256]{4,2,1,0,3:T(8,128)S(1)} %fusion.21, f32[4,8,34,3,256]{4,2,1,0,3:T(8,128)} %fusion.22, f32[4,8,34,3,256]{4,2,1,0,3:T(8,128)} %fusion.23, f32[4,8,34,3,256]{4,2,3,1,0:T(8,128)} %fusion.19, f32[4,8,34,3,256]{4,2,3,1,0:T(8,128)S(1)} %fusion.16, ...), kind=kLoop, calls=%fused_computation.35 | loop fusion | flops 7602176 | bytes 28836868 | tf_op jit(solution)/shard_map/convert_element_type | solution.py:147
  (92 shorter events, 28.2 us)
Async XLA Ops:
  19.0 49.7 %copy-start.9 = (s32[4]{0:T(128)S(1)}, s32[4]{0:T(128)}, u32[]{:S(2)}) copy-start(s32[4]{0:T(128)} %param.11) | copy-start | bytes 52
  19.0 46.4 %all-to-all-start.1 = ((bf16[4,8,48,512]{3,2,0,1:T(8,128)(2,1)}), bf16[4,8,48,512]{3,2,0,1:T(8,128)(2,1)S(1)}, u32[]{:S(2)}, u32[]{:S(2)}) async-start(bf16[4,8,48,512]{3,2,0,1:T(8,128)(2,1)} %copy.64), calls=%async_computation.1 | async-start | bytes 3145728 | tf_op jit(solution)/shard_map/all_to_all | solution.py:90
  31.0 21.8 %collective-permute-start.1 = (s32[4,1,48]{2,1,0:T(1,128)S(1)}, s32[4,1,48]{2,1,0:T(1,128)S(1)}, u32[]{:S(2)}, u32[]{:S(2)}) collective-permute-start(s32[4,1,48]{2,1,0:T(1,128)S(1)} %get-tuple-element.27), channel_id=1, source_target_pairs={{0,8},{4,12},{8,0},{12,4},{16,24},{20,28},{24,16},{28,20},{1,9},{5... | collective-permute-start | bytes 2312 | tf_op jit(solution)/shard_map/ppermute | solution.py:56
  33.0 22.6 %collective-permute-start = (s32[4,1,48]{2,1,0:T(1,128)S(1)}, s32[4,1,48]{2,1,0:T(1,128)S(1)}, u32[]{:S(2)}, u32[]{:S(2)}) collective-permute-start(s32[4,1,48]{2,1,0:T(1,128)S(1)} %get-tuple-element.28), channel_id=1, source_target_pairs={{0,4},{4,0},{8,12},{12,8},{16,20},{20,16},{24,28},{28,24},{1,5},{5... | collective-permute-start | bytes 2312 | tf_op jit(solution)/shard_map/ppermute | solution.py:56
  34.5 30.0 %collective-permute-start.4 = (s32[4,1,48]{2,1,0:T(1,128)S(1)}, s32[4,1,48]{2,1,0:T(1,128)S(1)}, u32[]{:S(2)}, u32[]{:S(2)}) collective-permute-start(s32[4,1,48]{2,1,0:T(1,128)S(1)} %get-tuple-element.24), channel_id=1, source_target_pairs={{0,20},{4,16},{8,28},{12,24},{16,4},{20,0},{24,12},{28,8},{1,21},{... | collective-permute-start | bytes 2312 | tf_op jit(solution)/shard_map/ppermute | solution.py:56
  36.9 20.4 %collective-permute-start.2 = (s32[4,1,48]{2,1,0:T(1,128)S(1)}, s32[4,1,48]{2,1,0:T(1,128)S(1)}, u32[]{:S(2)}, u32[]{:S(2)}) collective-permute-start(s32[4,1,48]{2,1,0:T(1,128)S(1)} %get-tuple-element.26), channel_id=1, source_target_pairs={{0,12},{4,8},{8,4},{12,0},{16,28},{20,24},{24,20},{28,16},{1,13},{... | collective-permute-start | bytes 2312 | tf_op jit(solution)/shard_map/ppermute | solution.py:56
  38.3 25.3 %collective-permute-start.3 = (s32[4,1,48]{2,1,0:T(1,128)S(1)}, s32[4,1,48]{2,1,0:T(1,128)S(1)}, u32[]{:S(2)}, u32[]{:S(2)}) collective-permute-start(s32[4,1,48]{2,1,0:T(1,128)S(1)} %get-tuple-element.25), channel_id=1, source_target_pairs={{0,16},{4,20},{8,24},{12,28},{16,0},{20,4},{24,8},{28,12},{1,17},{... | collective-permute-start | bytes 2312 | tf_op jit(solution)/shard_map/ppermute | solution.py:56
  52.8 11.8 %collective-permute-start.5 = (s32[4,1,48]{2,1,0:T(1,128)S(1)}, s32[4,1,48]{2,1,0:T(1,128)S(1)}, u32[]{:S(2)}, u32[]{:S(2)}) collective-permute-start(s32[4,1,48]{2,1,0:T(1,128)S(1)} %get-tuple-element.23), channel_id=1, source_target_pairs={{0,24},{4,28},{8,16},{12,20},{16,8},{20,12},{24,0},{28,4},{1,25},{... | collective-permute-start | bytes 2312 | tf_op jit(solution)/shard_map/ppermute | solution.py:56
  55.7 8.9 %collective-permute-start.6 = (s32[4,1,48]{2,1,0:T(1,128)S(1)}, s32[4,1,48]{2,1,0:T(1,128)S(1)}, u32[]{:S(2)}, u32[]{:S(2)}) collective-permute-start(s32[4,1,48]{2,1,0:T(1,128)S(1)} %get-tuple-element.22), channel_id=1, source_target_pairs={{0,28},{4,24},{8,20},{12,16},{16,12},{20,8},{24,4},{28,0},{1,29},{... | collective-permute-start | bytes 2312 | tf_op jit(solution)/shard_map/ppermute | solution.py:56
  65.3 7.0 %all-to-all-start = ((s32[4,1,384]{2,1,0:T(1,128)}), s32[4,1,384]{2,1,0:T(1,128)S(1)}, u32[]{:S(2)}, u32[]{:S(2)}) async-start(s32[4,1,384]{2,1,0:T(1,128)} %reshape.525), calls=%async_computation | async-start | bytes 12288 | tf_op jit(solution)/shard_map/all_to_all | solution.py:96
  72.3 29.3 %all-to-all-start.2 = ((bf16[4,8,48,512]{3,2,1,0:T(8,128)(2,1)}), bf16[4,8,48,512]{3,2,1,0:T(8,128)(2,1)}, u32[]{:S(2)}, u32[]{:S(2)}) async-start(bf16[4,8,48,512]{3,2,1,0:T(8,128)(2,1)} %copy.65), calls=%async_computation.2 | async-start | bytes 3145728 | tf_op jit(solution)/shard_map/all_to_all | solution.py:89
  101.6 45.8 %copy-start.6 = (f32[512]{0:T(512)S(1)}, f32[512]{0:T(512)}, u32[]{:S(2)}) copy-start(f32[512]{0:T(512)} %param.13) | copy-start | bytes 6148
  101.7 45.8 %copy-start.7 = (f32[512]{0:T(512)S(1)}, f32[512]{0:T(512)}, u32[]{:S(2)}) copy-start(f32[512]{0:T(512)} %param.12) | copy-start | bytes 6148
  110.9 25.7 %collective-permute-start.7 = (bf16[4,8,1,512]{3,2,1,0:T(2,128)(2,1)S(1)}, bf16[4,8,1,512]{3,2,1,0:T(2,128)(2,1)S(1)}, u32[]{:S(2)}, u32[]{:S(2)}) collective-permute-start(bf16[4,8,1,512]{3,2,1,0:T(2,128)(2,1)S(1)} %get-tuple-element.20), channel_id=1, source_target_pairs={{0,4},{4,8},{8,12},{12,16},{16,20},{20,24},{24,28},{1,5},{5,9},{9,... | collective-permute-start | bytes 98312 | tf_op jit(solution)/shard_map/ppermute | solution.py:18
  114.1 22.6 %collective-permute-start.8 = (bf16[4,8,1,512]{3,2,1,0:T(2,128)(2,1)S(1)}, bf16[4,8,1,512]{3,2,1,0:T(2,128)(2,1)S(1)}, u32[]{:S(2)}, u32[]{:S(2)}) collective-permute-start(bf16[4,8,1,512]{3,2,1,0:T(2,128)(2,1)S(1)} %get-tuple-element.21), channel_id=1, source_target_pairs={{4,0},{8,4},{12,8},{16,12},{20,16},{24,20},{28,24},{5,1},{9,5},{13... | collective-permute-start | bytes 98312 | tf_op jit(solution)/shard_map/ppermute | solution.py:18
  136.8 4.2 %collective-permute-start.9 = (bf16[4,1,34,512]{3,2,1,0:T(8,128)(2,1)S(1)}, bf16[4,1,34,512]{3,2,1,0:T(8,128)(2,1)S(1)}, u32[]{:S(2)}, u32[]{:S(2)}) collective-permute-start(bf16[4,1,34,512]{3,2,1,0:T(8,128)(2,1)S(1)} %get-tuple-element.18), channel_id=1, source_target_pairs={{0,16},{4,20},{8,24},{12,28},{1,17},{5,21},{9,25},{13,29},{2,18},{... | collective-permute-start | bytes 417800 | tf_op jit(solution)/shard_map/ppermute | solution.py:18
  138.2 9.2 %collective-permute-start.10 = (bf16[4,1,34,512]{3,2,1,0:T(8,128)(2,1)S(1)}, bf16[4,1,34,512]{3,2,1,0:T(8,128)(2,1)S(1)}, u32[]{:S(2)}, u32[]{:S(2)}) collective-permute-start(bf16[4,1,34,512]{3,2,1,0:T(8,128)(2,1)S(1)} %get-tuple-element.19), channel_id=1, source_target_pairs={{16,0},{20,4},{24,8},{28,12},{17,1},{21,5},{25,9},{29,13},{18,2},{... | collective-permute-start | bytes 417800 | tf_op jit(solution)/shard_map/ppermute | solution.py:18
  149.9 2.5 %copy-start.3 = (bf16[1,1,512,3,256]{2,4,3,1,0:T(8,128)(2,1)S(1)}, bf16[1,1,512,3,256]{2,4,3,1,0:T(8,128)(2,1)}, u32[]{:S(2)}) copy-start(bf16[1,1,512,3,256]{2,4,3,1,0:T(8,128)(2,1)} %copy.104) | copy-start | bytes 2359300
  152.4 1.3 copy-start.2
  154.9 1.3 copy-start.1
  156.2 1.3 copy-start
  157.4 3.1 %copy-start.5 = (bf16[1,1,512,3,256]{2,4,3,1,0:T(8,128)(2,1)S(1)}, bf16[1,1,512,3,256]{2,4,3,1,0:T(8,128)(2,1)}, u32[]{:S(2)}) copy-start(bf16[1,1,512,3,256]{2,4,3,1,0:T(8,128)(2,1)} %copy.110) | copy-start | bytes 2359300
  160.6 3.1 %copy-start.4 = (bf16[1,1,512,3,256]{2,4,3,1,0:T(8,128)(2,1)S(1)}, bf16[1,1,512,3,256]{2,4,3,1,0:T(8,128)(2,1)}, u32[]{:S(2)}) copy-start(bf16[1,1,512,3,256]{2,4,3,1,0:T(8,128)(2,1)} %copy.111) | copy-start | bytes 2359300
  167.0 3.2 %copy-start.8 = (f32[256]{0:T(256)S(1)}, f32[256]{0:T(256)}, u32[]{:S(2)}) copy-start(f32[256]{0:T(256)} %param.15) | copy-start | bytes 3076
